TPU v7x, 32 devices: a whole 2x2x4 slice. The times are simulated.
32 devices in a mesh: gx: 8 (over y, x, core), gy: 4 (over z).
Axes of the slice: x: 2, y: 2, z: 4, core: 2. Of those that a mesh axis runs over, the one named last changes fastest.
Arguments:
- dual_ops: float32 [8, 4, 1536, 1536], P('gx', 'gy')
- loads: float32 [8, 4, 2, 384, 128], P('gx', 'gy'), may hold values from -16 to 16
- coarse_rhs: float32 [8, 4, 6, 128], P('gx', 'gy'), may hold values from -288 to 288
- coarse_modes: float32 [8, 4, 2, 2, 6, 384], P('gx', 'gy'), as said below
- free_mask: int32 [8, 4, 2, 384], P('gx', 'gy'), may hold values from 0 to 1
- face_match: int32 [8, 4, 2, 384], P('gx', 'gy'), may hold values from 0 to 383, each once within a row
- coarse_rows: float32 [8, 4, 3, 6, 192], P('gx', 'gy'), as said below
Outputs:
- multipliers: float32 [8, 4, 2, 384, 128], P('gx', 'gy')
- projected: float32 [8, 4, 2, 384, 128], P('gx', 'gy')
Inputs may be any that keep to these rules, and one draw needn't show every extreme that they name: The draws of coarse_modes, free_mask and coarse_rows belong together. coarse_modes[a,b,0,1] is zero on the last grid column and coarse_modes[a,b,1,1] on the last grid row. With C the symmetric positive definite coarse matrix whose entries are the sums of free times products of the coarse-mode images of two modes over all east and south face multipliers (G^T G restricted to free multipliers, in the order (a, b, mode)), coarse_rows[a,b,0] are the rows of the inverse of C for the modes of (a,b), up to rounding; coarse_rows[a,b,1] equals coarse_rows[a,b+1,0] and coarse_rows[a,b,2] equals coarse_rows[a+1,b,0], zero where that neighbour does not exist.
All inputs are finite; a program needn't handle non-finite values.
Results may differ from a plain program's by a relative error of at most 0.00029.
Values sent between devices are 32-bit elements; how exact they have to be, the bound alone decides.
A program may use at most 64 MiB of HBM per device.

v0:
```python
import jax
import jax.numpy as jnp
from jax import lax
from jax.sharding import PartitionSpec as P

ITERS = 3


HIGHEST = lax.Precision.HIGHEST


def shifted(shard, axis, by):
    peers = lax.axis_size(axis)
    pairs = [(i, i + by) for i in range(peers) if 0 <= i + by < peers]
    return lax.ppermute(shard, axis, pairs)


def lower_shift(values, dimension):
    widths = [(0, 0)] * values.ndim
    widths[dimension] = (1, 0)
    return lax.slice_in_dim(jnp.pad(values, widths), 0, values.shape[dimension], axis=dimension)


def local(dual_ops, loads, coarse_rhs, coarse_modes, free_mask, face_match, coarse_rows):
    operator = dual_ops[0, 0]
    mode_table = coarse_modes[0, 0]
    free_slots = free_mask[0, 0].astype(jnp.float32)[..., None]
    slot_match = face_match[0, 0]
    inverse_rows = coarse_rows[0, 0]
    face_slots = slot_match.shape[1]
    case_count = loads.shape[-1]
    slot_order = jnp.arange(face_slots, dtype=jnp.int32)
    inverse_west = jnp.zeros((face_slots,), jnp.int32).at[slot_match[0]].set(slot_order)
    inverse_north = jnp.zeros((face_slots,), jnp.int32).at[slot_match[1]].set(slot_order)

    def apply_dual(field):
        from_west = shifted(field[0], "gy", 1)
        from_north = shifted(field[1], "gx", 1)
        west_side = -jnp.take(from_west, slot_match[0], axis=0)
        north_side = -jnp.take(from_north, slot_match[1], axis=0)
        stacked = jnp.concatenate([field[0], field[1], west_side, north_side], axis=0)
        product = jnp.dot(operator, stacked, precision=HIGHEST, preferred_element_type=jnp.float32)
        product = product.reshape(4, face_slots, case_count)
        back_west = shifted(jnp.take(product[2], inverse_west, axis=0), "gy", -1)
        back_north = shifted(jnp.take(product[3], inverse_north, axis=0), "gx", -1)
        return (product[:2] - jnp.stack([back_west, back_north])) * free_slots

    def coarse_terms(field):
        own_terms = jnp.einsum("fjk,fkc->jc", mode_table[:, 0], field, precision=HIGHEST)
        east_terms = jnp.dot(
            mode_table[0, 1], field[0], precision=HIGHEST, preferred_element_type=jnp.float32
        )
        south_terms = jnp.dot(
            mode_table[1, 1], field[1], precision=HIGHEST, preferred_element_type=jnp.float32
        )
        return (own_terms, east_terms, south_terms)

    def coarse_solve(own_terms, east_terms, south_terms):
        stacked = jnp.stack([own_terms, east_terms, south_terms])[None]
        gathered = lax.all_gather(stacked, ("gx", "gy"), axis=0, tiled=True)
        table = gathered.reshape(lax.axis_size("gx"), lax.axis_size("gy"), 3, 6, case_count)
        summed = table[:, :, 0] + lower_shift(table[:, :, 1], 1) + lower_shift(table[:, :, 2], 0)
        flat = summed.reshape(-1, case_count)
        return jnp.einsum("rjn,nc->rjc", inverse_rows, flat, precision=HIGHEST)

    def mode_images(alpha):
        east_face = jnp.einsum("jk,jc->kc", mode_table[0, 0], alpha[0], precision=HIGHEST)
        east_face = east_face + jnp.einsum(
            "jk,jc->kc", mode_table[0, 1], alpha[1], precision=HIGHEST
        )
        south_face = jnp.einsum("jk,jc->kc", mode_table[1, 0], alpha[0], precision=HIGHEST)
        south_face = south_face + jnp.einsum(
            "jk,jc->kc", mode_table[1, 1], alpha[2], precision=HIGHEST
        )
        return jnp.stack([east_face, south_face]) * free_slots

    def project(field):
        own_terms, east_terms, south_terms = coarse_terms(field)
        return field - mode_images(coarse_solve(own_terms, east_terms, south_terms))

    zeros_rhs = jnp.zeros_like(coarse_rhs[0, 0])
    multipliers = mode_images(coarse_solve(coarse_rhs[0, 0], zeros_rhs, zeros_rhs))
    gradient = apply_dual(multipliers) - loads[0, 0] * free_slots
    projected = project(gradient)
    norm_now = lax.psum(jnp.sum(projected * projected, axis=(0, 1)), ("gx", "gy"))
    direction = projected
    for step in range(ITERS):
        image = apply_dual(direction)
        projected_image = project(image)
        curvature, cross_term, image_square = lax.psum(
            (
                jnp.sum(direction * image, axis=(0, 1)),
                jnp.sum(projected * projected_image, axis=(0, 1)),
                jnp.sum(projected_image * projected_image, axis=(0, 1)),
            ),
            ("gx", "gy"),
        )
        step_size = norm_now / curvature
        multipliers = multipliers + step_size * direction
        projected = projected + step_size * projected_image
        if step + 1 < ITERS:
            norm_next = (
                norm_now + 2.0 * step_size * cross_term + step_size * step_size * image_square
            )
            direction = projected + norm_next / norm_now * direction
            norm_now = norm_next
    return (multipliers[None, None], projected[None, None])


def solution(mesh):
    in_specs = (
        P("gx", "gy", None, None),
        P("gx", "gy", None, None, None),
        P("gx", "gy", None, None),
        P("gx", "gy", None, None, None, None),
        P("gx", "gy", None, None),
        P("gx", "gy", None, None),
        P("gx", "gy", None, None, None),
    )
    out_specs = (P("gx", "gy", None, None, None), P("gx", "gy", None, None, None))
    return jax.shard_map(local, mesh=mesh, in_specs=in_specs, out_specs=out_specs, check_vma=False)
```

profile of v0, /device:TPU:0, one launch (start us, length us, event | category | flops | bytes accessed | tf_op | source)
XLA Modules:
  0.0 701.4 jit_solution(17421271332013993101)
XLA Ops:
  2.1 72.9 %all-gather = f32[96,6,128]{2,1,0:T(8,128)S(1)} all-gather(f32[3,6,128]{2,1,0:T(8,128)S(1)} %stack.195.clone), channel_id=2, replica_groups=mesh['gx'=8,'gy'=4] {'gx','gy'}, dimensions={0}, use_global_device_ids=true | all-gather | bytes 304128 | tf_op jit(solution)/shard_map/all_gather | solution.py:60
  78.7 1.3 collective-permute-start
  80.1 1.3 collective-permute-start.1
  82.2 2.9 scatter_custom_fusion.1
  86.0 2.9 scatter_custom_fusion
  90.6 1.1 gather_fusion.1
  91.9 12.2 %fusion.8 = f32[1536,128]{0,1:T(8,128)S(1)} fusion(f32[1,1,1536,1536]{3,2,1,0:T(8,128)} %param.9, f32[384,128]{0,1:T(8,128)S(1)} %select_negate_fusion.6, f32[384,128]{0,1:T(8,128)S(1)} %select_negate_fusion.7, f32[384,128]{0,1:T(8,128)S(1)} %get-tuple-element.74, f32[384,128]{0,1:T(8,128)S(1)} %get-tuple-element.73), kind=kOutput, calls=%fused_computation.26 | convolution fusion | flops 3624468480 | bytes 11010048 | tf_op jit(solution)/shard_map/dot_general | solution.py:42
  107.0 1.3 collective-permute-start.3
  108.3 1.8 collective-permute-start.2
  110.5 7.4 %collective-permute-done.2 = f32[384,128]{0,1:T(8,128)S(1)} collective-permute-done((f32[384,128]{0,1:T(8,128)S(1)}, f32[384,128]{0,1:T(8,128)S(1)}, u32[]{:S(2)}, u32[]{:S(2)}) %collective-permute-start.2) | collective-permute-done | bytes 196640 | tf_op jit(solution)/shard_map/ppermute | solution.py:15
  119.8 66.7 %all-gather.1 = f32[96,6,128]{2,1,0:T(8,128)S(1)} all-gather(f32[3,6,128]{2,1,0:T(8,128)S(1)} %pad_maximum_fusion.7), channel_id=3, replica_groups=mesh['gx'=8,'gy'=4] {'gx','gy'}, dimensions={0}, use_global_device_ids=true | all-gather | bytes 304128 | tf_op jit(solution)/shard_map/all_gather | solution.py:60
  189.3 3.8 collective-permute-start.4
  193.1 2.0 collective-permute-start.5
  195.1 1.2 collective-permute-done.4
  200.8 12.3 %fusion.11 = f32[1536,128]{0,1:T(8,128)S(1)} fusion(f32[1,1,1536,1536]{3,2,1,0:T(8,128)} %param.9, f32[384,128]{0,1:T(8,128)S(1)} %select_negate_fusion.4, f32[384,128]{0,1:T(8,128)} %select_negate_fusion.5, f32[384,128]{0,1:T(8,128)} %get-tuple-element.70, f32[384,128]{0,1:T(8,128)} %copy-done.16), kind=kOutput, calls=%fused_computation.27 | convolution fusion | flops 3624468480 | bytes 11010048 | tf_op jit(solution)/shard_map/dot_general | solution.py:42
  213.4 1.1 gather_fusion.6
  217.4 1.3 collective-permute-start.7
  218.7 1.3 collective-permute-start.6
  221.1 7.5 %collective-permute-done.6 = f32[384,128]{0,1:T(8,128)S(1)} collective-permute-done((f32[384,128]{0,1:T(8,128)}, f32[384,128]{0,1:T(8,128)S(1)}, u32[]{:S(2)}, u32[]{:S(2)}) %collective-permute-start.6) | collective-permute-done | bytes 196640 | tf_op jit(solution)/shard_map/ppermute | solution.py:15
  231.6 68.9 %all-gather.2 = f32[96,6,128]{2,1,0:T(8,128)S(1)} all-gather(f32[3,6,128]{2,1,0:T(8,128)S(1)} %pad_maximum_fusion.8), channel_id=4, replica_groups=mesh['gx'=8,'gy'=4] {'gx','gy'}, dimensions={0}, use_global_device_ids=true | all-gather | bytes 304128 | tf_op jit(solution)/shard_map/all_gather | solution.py:60
  303.3 1.9 copy.282
  305.2 1.9 copy.283
  307.1 2.1 multiply_reduce_fusion.5
  309.2 41.3 %all-reduce.12 = (f32[128]{0:T(128)S(1)}, f32[128]{0:T(128)S(1)}, f32[128]{0:T(128)S(1)}, f32[128]{0:T(128)S(1)}) all-reduce(f32[128]{0:T(128)S(1)} %get-tuple-element.15, f32[128]{0:T(128)S(1)} %get-tuple-element.17, f32[128]{0:T(128)S(1)} %get-tuple-element.16, ...), channel_id=1, replica_groups=mesh['gx'=8,'gy'=4] {'gx','gy'}, use_global_device_ids=true, to_apply=%region_9.11 | all-reduce | flops 512 | bytes 4096 | tf_op jit(solution)/shard_map/psum | solution.py:90
  352.5 1.8 collective-permute-start.8
  354.3 2.0 collective-permute-start.9
  356.3 1.4 collective-permute-done.8
  357.8 1.3 gather_fusion.8
  361.0 1.3 gather_fusion.9
  363.1 12.1 %fusion.14 = f32[1536,128]{0,1:T(8,128)S(1)} fusion(f32[1,1,1536,1536]{3,2,1,0:T(8,128)} %param.9, f32[384,128]{0,1:T(8,128)S(1)} %select_negate_fusion.2, f32[384,128]{0,1:T(8,128)S(1)} %select_negate_fusion.3, f32[384,128]{0,1:T(8,128)} %get-tuple-element.64, f32[384,128]{0,1:T(8,128)S(1)} %get-tuple-element.63), kind=kOutput, calls=%fused_computation.28 | convolution fusion | flops 3624468480 | bytes 11010048 | tf_op jit(solution)/shard_map/dot_general | solution.py:42
  379.0 1.3 collective-permute-start.11
  380.3 1.3 collective-permute-start.10
  381.6 1.9 collective-permute-done.11
  383.4 6.2 collective-permute-done.10
  390.4 1.1 copy.292
  392.4 2.0 subtract_multiply_fusion.3
  394.5 1.1 copy.297
  398.2 2.0 copy.332
  400.2 1.3 convolution_bitcast_fusion.14
  401.5 72.4 %all-gather.3 = f32[96,6,128]{2,1,0:T(8,128)S(1)} all-gather(f32[3,6,128]{2,1,0:T(8,128)S(1)} %pad_maximum_fusion.9), channel_id=5, replica_groups=mesh['gx'=8,'gy'=4] {'gx','gy'}, dimensions={0}, use_global_device_ids=true | all-gather | bytes 304128 | tf_op jit(solution)/shard_map/all_gather | solution.py:60
  478.2 1.9 copy.302
  480.1 1.9 copy.303
  482.0 2.3 multiply_reduce_fusion.2
  484.3 37.7 %all-reduce.11 = (f32[128]{0:T(128)S(1)}, f32[128]{0:T(128)S(1)}, f32[128]{0:T(128)S(1)}) all-reduce(f32[128]{0:T(128)S(1)} %get-tuple-element.13, f32[128]{0:T(128)S(1)} %get-tuple-element.12, f32[128]{0:T(128)S(1)} %get-tuple-element.11), channel_id=1, replica_groups=mesh['gx'=8,'gy'=4] {'gx','gy'}, use_global_device_ids=true, to_apply=%region_15.17 | all-reduce | flops 384 | bytes 3072 | tf_op jit(solution)/shard_map/psum | solution.py:90
  522.0 1.1 fusion.110
  523.1 1.3 multiply_add_fusion
  524.5 4.1 collective-permute-start.12
  528.6 2.0 collective-permute-start.13
  530.6 1.3 collective-permute-done.12
  537.1 12.2 %fusion.17 = f32[1536,128]{0,1:T(8,128)S(1)} fusion(f32[1,1,1536,1536]{3,2,1,0:T(8,128)} %param.9, f32[384,128]{0,1:T(8,128)S(1)} %select_negate_fusion, f32[384,128]{0,1:T(8,128)S(1)} %select_negate_fusion.1, f32[384,128]{0,1:T(8,128)} %copy-done.15, f32[384,128]{0,1:T(8,128)} %copy-done.14), kind=kOutput, calls=%fused_computation.29 | convolution fusion | flops 3624468480 | bytes 11010048 | tf_op jit(solution)/shard_map/dot_general | solution.py:42
  551.4 1.6 gather_fusion.14
  556.8 1.3 collective-permute-start.15
  558.1 1.3 collective-permute-start.14
  561.5 6.4 collective-permute-done.14
  570.0 3.1 multiply_reduce_fusion
  573.1 1.2 copy.316
  575.2 1.2 subtract_multiply_fusion
  577.0 2.0 copy.333
  579.0 1.3 convolution_bitcast_fusion.13
  580.3 70.8 %all-gather.4 = f32[96,6,128]{2,1,0:T(8,128)S(1)} all-gather(f32[3,6,128]{2,1,0:T(8,128)S(1)} %pad_maximum_fusion.10), channel_id=6, replica_groups=mesh['gx'=8,'gy'=4] {'gx','gy'}, dimensions={0}, use_global_device_ids=true | all-gather | bytes 304128 | tf_op jit(solution)/shard_map/all_gather | solution.py:60
  652.9 39.1 %psum.63 = f32[128]{0:T(128)S(1)} all-reduce(f32[128]{0:T(128)} %get-tuple-element.31), channel_id=1, replica_groups=mesh['gx'=8,'gy'=4] {'gx','gy'}, use_global_device_ids=true, to_apply=%region_17.19 | all-reduce | flops 128 | bytes 1024 | tf_op jit(solution)/shard_map/psum | solution.py:90
  692.9 1.3 fusion.20
  695.3 2.7 fusion.67
  698.9 1.4 fusion.52
  (272 shorter events, 69.5 us)
Async XLA Ops:
  78.7 10.3 %copy-start.6 = (f32[128,384]{1,0:T(8,128)}, f32[128,384]{1,0:T(8,128)S(1)}, u32[]{:S(2)}) copy-start(f32[128,384]{1,0:T(8,128)S(1)} %convolution_add_fusion.9) | copy-start | bytes 589828
  78.7 10.3 %collective-permute-start = (f32[384,128]{0,1:T(8,128)S(1)}, f32[384,128]{0,1:T(8,128)S(1)}, u32[]{:S(2)}, u32[]{:S(2)}) collective-permute-start(f32[384,128]{0,1:T(8,128)S(1)} %get-tuple-element.73), channel_id=1, source_target_pairs={{0,1},{1,2},{2,3},{4,5},{5,6},{6,7},{8,9},{9,10},{10,11},{12,13},{... | collective-permute-start | bytes 589832 | tf_op jit(solution)/shard_map/ppermute | solution.py:15
  80.1 10.4 %collective-permute-start.1 = (f32[384,128]{0,1:T(8,128)S(1)}, f32[384,128]{0,1:T(8,128)S(1)}, u32[]{:S(2)}, u32[]{:S(2)}) collective-permute-start(f32[384,128]{0,1:T(8,128)S(1)} %get-tuple-element.74), channel_id=1, source_target_pairs={{0,4},{4,8},{8,12},{12,16},{16,20},{20,24},{24,28},{1,5},{5,9},{9,... | collective-permute-start | bytes 589832 | tf_op jit(solution)/shard_map/ppermute | solution.py:15
  85.1 131.6 %copy-start.28 = (pred[384]{0:T(512)(128)(4,1)}, pred[384]{0:T(512)(128)(4,1)S(1)}, u32[]{:S(2)}) copy-start(pred[384]{0:T(512)(128)(4,1)S(1)} %compare_and_fusion) | copy-start | bytes 1156
  85.9 111.8 %copy-start.35 = (pred[384]{0:T(512)(128)(4,1)}, pred[384]{0:T(512)(128)(4,1)S(1)}, u32[]{:S(2)}) copy-start(pred[384]{0:T(512)(128)(4,1)S(1)} %get-tuple-element.81) | copy-start | bytes 1156
  85.9 114.8 %copy-start.31 = (pred[384]{0:T(512)(128)(4,1)}, pred[384]{0:T(512)(128)(4,1)S(1)}, u32[]{:S(2)}) copy-start(pred[384]{0:T(512)(128)(4,1)S(1)} %get-tuple-element.80) | copy-start | bytes 1156
  88.9 124.4 %copy-start.17 = (s32[1024]{0:T(1024)}, s32[1024]{0:T(1024)S(1)}, u32[]{:S(2)}) copy-start(s32[1024]{0:T(1024)S(1)} %pad_clamp_fusion.1) | copy-start | bytes 12292
  88.9 110.5 %copy-start.20 = (s32[1024]{0:T(1024)}, s32[1024]{0:T(1024)S(1)}, u32[]{:S(2)}) copy-start(s32[1024]{0:T(1024)S(1)} %pad_clamp_fusion.2) | copy-start | bytes 12292
  89.0 107.5 %copy-start.22 = (s32[1024]{0:T(1024)}, s32[1024]{0:T(1024)S(1)}, u32[]{:S(2)}) copy-start(s32[1024]{0:T(1024)S(1)} %pad_clamp_fusion.3) | copy-start | bytes 12292
  89.0 125.6 %copy-start.32 = (pred[384]{0:T(512)(128)(4,1)}, pred[384]{0:T(512)(128)(4,1)S(1)}, u32[]{:S(2)}) copy-start(pred[384]{0:T(512)(128)(4,1)S(1)} %compare_and_fusion.1) | copy-start | bytes 1156
  91.7 18.4 %copy-start.12 = (f32[1,1,2,384,128]{4,3,2,1,0:T(8,128)S(1)}, f32[1,1,2,384,128]{4,3,2,1,0:T(8,128)}, u32[]{:S(2)}) copy-start(f32[1,1,2,384,128]{4,3,2,1,0:T(8,128)} %param.10) | copy-start | bytes 1179652
  104.1 82.5 %copy-start.13 = (f32[1,1,3,6,192]{4,1,3,2,0:T(1,128)S(1)}, f32[1,1,3,6,192]{4,1,3,2,0:T(1,128)}, u32[]{:S(2)}) copy-start(f32[1,1,3,6,192]{4,1,3,2,0:T(1,128)} %param.15) | copy-start | bytes 41476
  107.0 3.5 collective-permute-start.3
  108.3 9.5 %collective-permute-start.2 = (f32[384,128]{0,1:T(8,128)S(1)}, f32[384,128]{0,1:T(8,128)S(1)}, u32[]{:S(2)}, u32[]{:S(2)}) collective-permute-start(f32[384,128]{0,1:T(8,128)S(1)} %broadcast_select_fusion.7), channel_id=1, source_target_pairs={{1,0},{2,1},{3,2},{5,4},{6,5},{7,6},{9,8},{10,9},{11,10},{13,12},{... | collective-permute-start | bytes 589832 | tf_op jit(solution)/shard_map/ppermute | solution.py:15
  110.3 90.4 %copy-start.2 = (f32[1,1,2,384,128]{3,4,2,1,0:T(8,128)}, f32[1,1,2,384,128]{3,4,2,1,0:T(8,128)S(1)}, u32[]{:S(2)}) copy-start(f32[1,1,2,384,128]{3,4,2,1,0:T(8,128)S(1)} %copy.257) | copy-start | bytes 1179652
  110.4 90.2 %copy-start.10 = (f32[384,128]{0,1:T(8,128)}, f32[384,128]{0,1:T(8,128)S(1)}, u32[]{:S(2)}) copy-start(f32[384,128]{0,1:T(8,128)S(1)} %collective-permute-done.3) | copy-start | bytes 589828
  117.8 82.8 %copy-start.11 = (f32[384,128]{0,1:T(8,128)}, f32[384,128]{0,1:T(8,128)S(1)}, u32[]{:S(2)}) copy-start(f32[384,128]{0,1:T(8,128)S(1)} %collective-permute-done.2) | copy-start | bytes 589828
  188.1 12.7 %copy-start.8 = (f32[128,384]{1,0:T(8,128)}, f32[128,384]{1,0:T(8,128)S(1)}, u32[]{:S(2)}) copy-start(f32[128,384]{1,0:T(8,128)S(1)} %convolution_add_fusion.6) | copy-start | bytes 589828
  188.5 12.3 %copy-start.9 = (f32[128,384]{1,0:T(8,128)}, f32[128,384]{1,0:T(8,128)S(1)}, u32[]{:S(2)}) copy-start(f32[128,384]{1,0:T(8,128)S(1)} %convolution_add_fusion.7) | copy-start | bytes 589828
  189.3 5.8 copy-start.16
  189.3 7.0 collective-permute-start.4
  193.1 5.3 collective-permute-start.5
  213.2 15.6 %copy-start.4 = (f32[1536,128]{0,1:T(8,128)}, f32[1536,128]{0,1:T(8,128)S(1)}, u32[]{:S(2)}) copy-start(f32[1536,128]{0,1:T(8,128)S(1)} %fusion.11) | copy-start | bytes 2359300
  217.4 3.7 collective-permute-start.7
  218.7 9.9 %collective-permute-start.6 = (f32[384,128]{0,1:T(8,128)}, f32[384,128]{0,1:T(8,128)S(1)}, u32[]{:S(2)}, u32[]{:S(2)}) collective-permute-start(f32[384,128]{0,1:T(8,128)} %broadcast_select_fusion.5), channel_id=1, source_target_pairs={{1,0},{2,1},{3,2},{5,4},{6,5},{7,6},{9,8},{10,9},{11,10},{13,12},{... | collective-permute-start | bytes 589832 | tf_op jit(solution)/shard_map/ppermute | solution.py:15
  351.0 0.6 copy-start.24
  351.0 24.2 %copy-start.26 = (f32[128]{0:T(128)}, f32[128]{0:T(128)S(1)}, u32[]{:S(2)}) copy-start(f32[128]{0:T(128)S(1)} %get-tuple-element.37) | copy-start | bytes 1540
  351.8 24.5 %copy-start.18 = (s32[1024]{0:T(1024)S(1)}, s32[1024]{0:T(1024)}, u32[]{:S(2)}) copy-start(s32[1024]{0:T(1024)} %copy-done.17) | copy-start | bytes 12292
  352.5 5.2 collective-permute-start.8
  354.3 5.6 collective-permute-start.9
  359.1 18.4 %copy-start.33 = (pred[384]{0:T(512)(128)(4,1)S(1)}, pred[384]{0:T(512)(128)(4,1)}, u32[]{:S(2)}) copy-start(pred[384]{0:T(512)(128)(4,1)} %copy-done.32) | copy-start | bytes 1156
  362.2 16.7 %copy-start.29 = (pred[384]{0:T(512)(128)(4,1)S(1)}, pred[384]{0:T(512)(128)(4,1)}, u32[]{:S(2)}) copy-start(pred[384]{0:T(512)(128)(4,1)} %copy-done.28) | copy-start | bytes 1156
  375.2 0.9 copy-start.5
  379.0 4.5 collective-permute-start.11
  380.3 9.3 %collective-permute-start.10 = (f32[384,128]{0,1:T(8,128)S(1)}, f32[384,128]{0,1:T(8,128)S(1)}, u32[]{:S(2)}, u32[]{:S(2)}) collective-permute-start(f32[384,128]{0,1:T(8,128)S(1)} %broadcast_select_fusion.3), channel_id=1, source_target_pairs={{1,0},{2,1},{3,2},{5,4},{6,5},{7,6},{9,8},{10,9},{11,10},{13,12},{... | collective-permute-start | bytes 589832 | tf_op jit(solution)/shard_map/ppermute | solution.py:15
  395.6 80.5 %copy-start = (f32[768,128]{1,0:T(8,128)}, f32[768,128]{1,0:T(8,128)S(1)}, u32[]{:S(2)}) copy-start(f32[768,128]{1,0:T(8,128)S(1)} %copy.297) | copy-start | bytes 1179652
  474.6 57.5 %copy-start.23 = (s32[1024]{0:T(1024)S(1)}, s32[1024]{0:T(1024)}, u32[]{:S(2)}) copy-start(s32[1024]{0:T(1024)} %copy-done.22) | copy-start | bytes 12292
  474.6 60.5 %copy-start.21 = (s32[1024]{0:T(1024)S(1)}, s32[1024]{0:T(1024)}, u32[]{:S(2)}) copy-start(s32[1024]{0:T(1024)} %copy-done.20) | copy-start | bytes 12292
  523.1 46.9 %copy-start.36 = (f32[128]{0:T(128)}, f32[128]{0:T(128)S(1)}, u32[]{:S(2)}) copy-start(f32[128]{0:T(128)S(1)} %get-tuple-element.35) | copy-start | bytes 1540
  523.1 46.9 %copy-start.38 = (f32[128]{0:T(128)}, f32[128]{0:T(128)S(1)}, u32[]{:S(2)}) copy-start(f32[128]{0:T(128)S(1)} %get-tuple-element.33) | copy-start | bytes 1540
  524.4 27.0 %copy-start.19 = (s32[1024]{0:T(1024)S(1)}, s32[1024]{0:T(1024)}, u32[]{:S(2)}) copy-start(s32[1024]{0:T(1024)} %copy-done.17) | copy-start | bytes 12292
  524.4 8.7 %copy-start.14 = (f32[384,128]{0,1:T(8,128)}, f32[384,128]{0,1:T(8,128)S(1)}, u32[]{:S(2)}) copy-start(f32[384,128]{0,1:T(8,128)S(1)} %get-tuple-element.59) | copy-start | bytes 589828
  524.4 11.8 %copy-start.15 = (f32[384,128]{0,1:T(8,128)}, f32[384,128]{0,1:T(8,128)S(1)}, u32[]{:S(2)}) copy-start(f32[384,128]{0,1:T(8,128)S(1)} %get-tuple-element.60) | copy-start | bytes 589828
  524.5 7.4 %collective-permute-start.12 = (f32[384,128]{0,1:T(8,128)S(1)}, f32[384,128]{0,1:T(8,128)S(1)}, u32[]{:S(2)}, u32[]{:S(2)}) collective-permute-start(f32[384,128]{0,1:T(8,128)S(1)} %get-tuple-element.59), channel_id=1, source_target_pairs={{0,1},{1,2},{2,3},{4,5},{5,6},{6,7},{8,9},{9,10},{10,11},{12,13},{... | collective-permute-start | bytes 589832 | tf_op jit(solution)/shard_map/ppermute | solution.py:15
  528.6 5.4 collective-permute-start.13
  533.2 20.9 %copy-start.34 = (pred[384]{0:T(512)(128)(4,1)S(1)}, pred[384]{0:T(512)(128)(4,1)}, u32[]{:S(2)}) copy-start(pred[384]{0:T(512)(128)(4,1)} %copy-done.32) | copy-start | bytes 1156
  536.2 19.9 %copy-start.30 = (pred[384]{0:T(512)(128)(4,1)S(1)}, pred[384]{0:T(512)(128)(4,1)}, u32[]{:S(2)}) copy-start(pred[384]{0:T(512)(128)(4,1)} %copy-done.28) | copy-start | bytes 1156
  537.0 23.4 %copy-start.1 = (f32[768,128]{1,0:T(8,128)S(1)}, f32[768,128]{1,0:T(8,128)}, u32[]{:S(2)}) copy-start(f32[768,128]{1,0:T(8,128)} %copy-done) | copy-start | bytes 1179652
  537.1 33.0 %copy-start.25 = (f32[128]{0:T(128)S(1)}, f32[128]{0:T(128)}, u32[]{:S(2)}) copy-start(f32[128]{0:T(128)} %copy-done.24) | copy-start | bytes 1540
  537.1 33.0 %copy-start.27 = (f32[128]{0:T(128)S(1)}, f32[128]{0:T(128)}, u32[]{:S(2)}) copy-start(f32[128]{0:T(128)} %copy-done.26) | copy-start | bytes 1540
  549.3 1.0 copy-start.3
  556.8 4.6 collective-permute-start.15
  558.1 9.8 %collective-permute-start.14 = (f32[384,128]{0,1:T(8,128)}, f32[384,128]{0,1:T(8,128)}, u32[]{:S(2)}, u32[]{:S(2)}) collective-permute-start(f32[384,128]{0,1:T(8,128)} %broadcast_select_fusion.1), channel_id=1, source_target_pairs={{1,0},{2,1},{3,2},{5,4},{6,5},{7,6},{9,8},{10,9},{11,10},{13,12},{... | collective-permute-start | bytes 589832 | tf_op jit(solution)/shard_map/ppermute | solution.py:15
  569.1 129.8 %copy-start.7 = (f32[128,384]{1,0:T(8,128)S(1)}, f32[128,384]{1,0:T(8,128)}, u32[]{:S(2)}) copy-start(f32[128,384]{1,0:T(8,128)} %copy-done.6) | copy-start | bytes 589828
  573.1 125.8 %copy-start.37 = (f32[128]{0:T(128)S(1)}, f32[128]{0:T(128)}, u32[]{:S(2)}) copy-start(f32[128]{0:T(128)} %copy-done.36) | copy-start | bytes 1540
  573.1 125.8 %copy-start.39 = (f32[128]{0:T(128)S(1)}, f32[128]{0:T(128)}, u32[]{:S(2)}) copy-start(f32[128]{0:T(128)} %copy-done.38) | copy-start | bytes 1540
where the time goes:
time: 711 us; the launch traced here: 701 us
  blocking collectives  470 us (66%)
  matrix products  67.2 us (9%)
  local copies, waits for them, and re-layouts  66.4 us (9%)
  waiting for transfers between devices  34.1 us (5%)
  other arithmetic  32.3 us (5%)
  starting transfers between devices  29.1 us (4%)
    all_gather x5, blocking collectives, coarse_solve(): gathered = lax.all_gather(stacked, ('gx', 'gy'), axis=0, tiled=True)  352 us
    psum x3, blocking collectives, local(): lax.psum((jnp.sum(direction * image, axis=(0, 1)), jnp.sum(projected * pr...  118 us
    dot_general x4, matrix products, apply_dual(): jnp.dot(operator, stacked, precision=HIGHEST, preferred_element_type=jnp....  48.9 us
    ppermute x16, waiting for transfers between devices, shifted(): return lax.ppermute(shard, axis, pairs)  34.1 us
    ppermute x16, starting transfers between devices, shifted(): return lax.ppermute(shard, axis, pairs)  29.1 us
  transfers between devices with their start and end apart: 16, of which 9 were waited for; matrix products, arithmetic and copies ran while one was open for 3% of the time, Pallas kernels for 0%

commit v1 on v0

v1 whole, which is shorter than its diff:
```python
import functools

import jax
import jax.numpy as jnp
from jax import lax
from jax.experimental import pallas as pl
from jax.experimental.pallas import tpu as pltpu
from jax.sharding import PartitionSpec as P

ITERS = 3
F32 = jnp.float32
BF16 = jnp.bfloat16
MESH = pl.DeviceIdType.MESH
EAST, SOUTH, WEST, NORTH = 0, 1, 2, 3
OPPOSITE = (WEST, NORTH, EAST, SOUTH)
ROUNDS = ITERS + 2
APPLIES = ITERS + 1


def split(values):
    high = values.astype(BF16)
    low = (values - high.astype(F32)).astype(BF16)
    return high, low


def dot32(left, right):
    return jnp.dot(left, right, preferred_element_type=F32)


def kernel(
    nx, ny, a_hbm, loads_hbm, rhs_ref, modes_ref, free_ref, match_ref, rows_ref,
    mult_ref, proj_ref,
    a_stage, a_high, a_low, loads4, pack, nb_pack, inverse, terms, alphas, alpha_pair,
    gt8, g_high, g_low, fg_high, fg_low, free4, put, perm, perm_back, vsplit, u_split,
    outbox, inbox, p_f, d_f, q_f, fp_f, fq_f,
    a_sem, l_sem, face_send, face_recv, pk_send, pk_recv, ld_send, ld_recv,
    gy_send, gy_recv, gx_send, gx_recv, cy_send, cy_recv, cx_send, cx_recv,
):
    lf = free_ref.shape[1]
    nc = mult_ref.shape[1]
    lm = a_high.shape[0]
    ncoarse = rows_ref.shape[2]
    wide = inverse.shape[3]
    me_x = lax.axis_index("gx")
    me_y = lax.axis_index("gy")
    exists = (me_y < ny - 1, me_x < nx - 1, me_y > 0, me_x > 0)
    place = ((me_x, me_y + 1), (me_x + 1, me_y), (me_x, me_y - 1), (me_x - 1, me_y))

    def face(f):
        return pl.ds(f * lf, lf)

    chunk = lm // 6
    a_copies = [
        pltpu.make_async_copy(
            a_hbm.at[pl.ds(i * chunk, chunk)], a_stage.at[pl.ds(i * chunk, chunk)], a_sem.at[i]
        )
        for i in range(6)
    ]
    for copy in a_copies:
        copy.start()
    l_copy = pltpu.make_async_copy(loads_hbm, loads4.at[pl.ds(0, 2 * lf)], l_sem)
    l_copy.start()

    barrier = pltpu.get_barrier_semaphore()
    for t in range(1, nx):
        pl.semaphore_signal(
            barrier, inc=1, device_id=(lax.rem(me_x + t, nx), me_y), device_id_type=MESH
        )
    for t in range(1, ny):
        pl.semaphore_signal(
            barrier, inc=1, device_id=(me_x, lax.rem(me_y + t, ny)), device_id_type=MESH
        )

    pack[...] = jnp.zeros_like(pack)
    for f in range(2):
        pack[f, 0:6, :] = modes_ref[f, 0]
        pack[f, 8:14, :] = modes_ref[f, 1]
        pack[f, 16:17, :] = free_ref[f : f + 1, :].astype(F32)

    row = lax.broadcasted_iota(jnp.int32, (ncoarse, wide), 0)
    col = lax.broadcasted_iota(jnp.int32, (ncoarse, wide), 1)
    slot = jnp.bitwise_and(col, 7)
    spread = jnp.where((row == 6 * jnp.right_shift(col, 3) + slot) & (slot < 6), 1.0, 0.0)
    inverse[me_x, me_y] = jnp.zeros((8, wide), F32)
    inverse[me_x, me_y, 0:6, :] = jnp.dot(
        rows_ref[0], spread.astype(F32), precision=lax.Precision.HIGHEST,
        preferred_element_type=F32,
    )
    terms[0, me_x, me_y] = jnp.zeros((16, nc), F32)
    terms[0, me_x, me_y, 0:6, :] = rhs_ref[...]

    pl.semaphore_wait(barrier, nx + ny - 2)

    def remote(src, dst, send, recv, where):
        return pltpu.make_async_remote_copy(
            src_ref=src, dst_ref=dst, send_sem=send, recv_sem=recv,
            device_id=where, device_id_type=MESH,
        )

    def neighbour_copy(f, src, dst, send, recv):
        return remote(src, dst, send, recv, place[f])

    for f in range(2):
        @pl.when(exists[f])
        def _():
            neighbour_copy(f, pack.at[f], nb_pack.at[f], pk_send.at[f], pk_recv.at[f]).start()

    def spread_column(view, send, recv):
        copies = []
        for t in range(1, ny):
            copies.append(remote(
                view(me_x, me_y), view(me_x, me_y), send.at[t], recv.at[t],
                (me_x, lax.rem(me_y + t, ny)),
            ))
        return copies

    def spread_row(view, send, recv):
        copies = []
        for t in range(1, nx):
            copies.append(remote(
                view(me_x), view(me_x), send.at[t], recv.at[t],
                (lax.rem(me_x + t, nx), me_y),
            ))
        return copies

    pending = []

    def begin(copies):
        for copy in copies:
            copy.start()
        pending.extend(copies)

    def finish(copies):
        for copy in copies:
            copy.wait_recv()

    def terms_column(r, rows):
        return spread_column(
            lambda x, y: terms.at[r, x, y, pl.ds(0, rows)], gy_send.at[r], gy_recv.at[r]
        )

    def terms_row(r, rows):
        return spread_row(
            lambda x: terms.at[r, x, :, pl.ds(0, rows)], gx_send.at[r], gx_recv.at[r]
        )

    inv_col = spread_column(lambda x, y: inverse.at[x, y], cy_send, cy_recv)
    inv_row = spread_row(lambda x: inverse.at[x], cx_send, cx_recv)
    rhs_col = terms_column(0, 8)
    rhs_row = terms_row(0, 8)
    begin(rhs_col)
    begin(inv_col)
    for f in range(2):
        @pl.when(exists[f])
        def _():
            neighbour_copy(
                f, loads_hbm.at[face(f)], loads4.at[face(2 + f)], ld_send.at[f], ld_recv.at[f]
            ).start()

    for f in range(4):
        @pl.when(jnp.logical_not(exists[f]))
        def _():
            for r in range(APPLIES):
                inbox[r, f] = jnp.zeros((lf, nc), F32)
    for f in range(2):
        @pl.when(jnp.logical_not(exists[2 + f]))
        def _():
            nb_pack[f] = jnp.zeros((24, lf), F32)
            loads4[face(2 + f), :] = jnp.zeros((lf, nc), F32)

    slots = lax.broadcasted_iota(jnp.int32, (lf, lf), 0)
    for f in range(2):
        back = jnp.where(slots == match_ref[f : f + 1, :], 1.0, 0.0).astype(F32)
        perm_back[f] = back.astype(BF16)
        perm[f] = (-jnp.transpose(back)).astype(BF16)

    def cast_chunk(i):
        a_copies[i].wait()
        part = a_stage[pl.ds(i * chunk, chunk), :]
        high, low = split(part)
        a_high[pl.ds(i * chunk, chunk), :] = high
        a_low[pl.ds(i * chunk, chunk), :] = low

    for i in range(3):
        cast_chunk(i)

    finish(rhs_col)
    begin(rhs_row)
    finish(inv_col)
    begin(inv_row)

    for i in range(3, 6):
        cast_chunk(i)

    for f in range(2):
        @pl.when(exists[2 + f])
        def _():
            neighbour_copy(f, pack.at[f], nb_pack.at[f], pk_send.at[f], pk_recv.at[f]).wait_recv()

    for f in range(4):
        put[...] = jnp.zeros_like(put)
        source = pack if f < 2 else nb_pack
        mask = source[f % 2, 16:17, :]
        owner = source[f % 2, 0:8, :] * mask
        other = source[f % 2, 8:16, :] * mask
        own_part, far_part = (owner, other) if f < 2 else (other, owner)
        put[0:8, :] = own_part
        put[8 * (f + 1) : 8 * (f + 2), :] = far_part
        high, low = split(own_part)
        gt8[0:8, face(f)] = high.astype(F32)
        gt8[8:16, face(f)] = low.astype(F32)
        q_f[face(f), :] = jnp.transpose(put[...])
        free4[face(f), :] = jnp.transpose(jnp.broadcast_to(mask, (nc, lf)))
    high, low = split(q_f[...])
    g_high[...] = high
    g_low[...] = low

    def split_field(ref):
        high, low = split(ref[...])
        vsplit[:, 0:nc] = high
        vsplit[:, nc : 2 * nc] = low

    def coarse_terms(r):
        both = dot32(gt8[...].astype(BF16), vsplit[...])
        terms[r, me_x, me_y, 0:8, :] = (
            both[0:8, 0:nc] + both[0:8, nc : 2 * nc] + both[8:16, 0:nc]
        )
        terms[r, me_x, me_y, 8:16, :] = jnp.zeros((8, nc), F32)

    def face_copy(r, f):
        g = OPPOSITE[f]
        return neighbour_copy(
            f, outbox.at[r, f], inbox.at[r, g], face_send.at[r, f], face_recv.at[r, g]
        )

    def apply_start(r, between):
        u_split[face(EAST), :] = vsplit[face(EAST), :]
        u_split[face(SOUTH), :] = vsplit[face(SOUTH), :]
        for f in range(2):
            u_split[face(2 + f), :] = dot32(perm[f], vsplit[face(2 + f), :]).astype(BF16)
        for f in (WEST, EAST, NORTH, SOUTH):
            both = dot32(a_high[face(f), :], u_split[...])
            z = dot32(a_low[face(f), :], u_split[:, 0:nc])
            z = z + both[:, 0:nc] + both[:, nc : 2 * nc]
            if f >= 2:
                high, low = split(z)
                z = dot32(perm_back[f - 2], high) + dot32(perm_back[f - 2], low)
            outbox[r, f] = z

            @pl.when(exists[f])
            def _():
                face_copy(r, f).start()

            if f == EAST:
                between()

    def face_arrived(r, f):
        g = OPPOSITE[f]

        @pl.when(exists[f])
        def _():
            remote(
                outbox.at[r, g], inbox.at[r, f], face_send.at[r, g], face_recv.at[r, f], place[f]
            ).wait_recv()

    def apply_finish(r, out):
        for f in (EAST, WEST, SOUTH, NORTH):
            face_arrived(r, f)
            delta = outbox[r, f] - inbox[r, f] if f < 2 else inbox[r, f] - outbox[r, f]
            out[face(f), :] = delta * free4[face(f), :]

    def solve(r):
        c = terms[r, :, :, 0:8, :].reshape(nx * ny * 8, nc)
        full = inverse[...].reshape(nx * ny * 8, wide)
        alpha = jnp.dot(
            full, c, precision=lax.Precision.HIGHEST, preferred_element_type=F32
        )
        alphas[...] = alpha.reshape(nx * ny, 8, nc)
        fill(0, me_x, me_y)
        for f in range(4):
            fill(f + 1, *place[f])
        return jnp.sum(c * alpha, axis=0, keepdims=True)

    def fill(which, x, y):
        for k, (dx, dy) in enumerate(((0, 0), (0, 1), (1, 0), (0, -1), (-1, 0))):
            xx = jnp.clip(x + dx, 0, nx - 1)
            yy = jnp.clip(y + dy, 0, ny - 1)
            high, low = split(alphas[xx * ny + yy])
            alpha_pair[which, 8 * k : 8 * k + 8, 0:nc] = high.astype(F32)
            alpha_pair[which, 8 * k : 8 * k + 8, nc : 2 * nc] = low.astype(F32)

    def product(left_high, left_low, right):
        both = dot32(left_high, right)
        return dot32(left_low, right[:, 0:nc]) + both[:, 0:nc] + both[:, nc : 2 * nc]

    def mode_image(f):
        return product(
            g_high[face(f), :], g_low[face(f), :], alpha_pair[0].astype(BF16)
        )

    def dual_mode_image(f):
        right = jnp.concatenate([alpha_pair[0], alpha_pair[f + 1]], axis=0).astype(BF16)
        return product(fg_high[face(f), :], fg_low[face(f), :], right)

    def own_sum(left, right):
        return jnp.sum(
            left[0 : 2 * lf, :] * right[0 : 2 * lf, :], axis=0, keepdims=True
        )

    def totals(r, rows):
        return jnp.sum(terms[r, :, :, 0:rows, :].reshape(nx * ny, rows, nc), axis=0)

    alpha_pair[...] = jnp.zeros_like(alpha_pair)

    vsplit[:, 0:nc] = g_high[...]
    vsplit[:, nc : 2 * nc] = g_low[...]
    apply_start(0, lambda: None)
    finish(rhs_row)
    finish(inv_row)
    solve(0)
    for f in range(2):
        mult_ref[face(f), :] = mode_image(f)
    for f in (EAST, WEST, SOUTH, NORTH):
        face_arrived(0, f)
        sign = 1.0 if f < 2 else -1.0
        mask = free4[face(f), :] * sign
        for half, values in enumerate((outbox[0, f] * mask, -inbox[0, f] * mask)):
            high, low = split(values)
            fg_high[face(f), half * nc : (half + 1) * nc] = high
            fg_low[face(f), half * nc : (half + 1) * nc] = low

    l_copy.wait()
    for f in range(2):
        @pl.when(exists[2 + f])
        def _():
            neighbour_copy(
                f, loads_hbm.at[face(f)], loads4.at[face(2 + f)], ld_send.at[f], ld_recv.at[f]
            ).wait_recv()
    for f in range(4):
        p_f[face(f), :] = dual_mode_image(f) - loads4[face(f), :] * free4[face(f), :]

    def round_trip(r, rows, apply, out):
        column = terms_column(r, rows)
        line = terms_row(r, rows)
        begin(column)

        def relay():
            finish(column)
            begin(line)

        if apply:
            apply_start(r, relay)
            finish(line)
        else:
            relay()
            finish(line)
        inner = solve(r)
        if apply:
            apply_finish(r, out)
        return inner

    split_field(p_f)
    coarse_terms(1)
    round_trip(1, 8, True, q_f)
    for f in range(4):
        p = p_f[face(f), :] - mode_image(f)
        p_f[face(f), :] = p
        d_f[face(f), :] = p
        q = q_f[face(f), :] - dual_mode_image(f)
        q_f[face(f), :] = q
        fp_f[face(f), :] = q

    norm = None
    for step in range(ITERS):
        r = step + 2
        last = step + 1 == ITERS
        split_field(q_f)
        coarse_terms(r)
        rows = 8 if last else 16
        terms[r, me_x, me_y, 6:7, :] = own_sum(d_f, q_f)
        if not last:
            terms[r, me_x, me_y, 7:8, :] = own_sum(p_f, p_f if step == 0 else q_f)
            terms[r, me_x, me_y, 8:9, :] = own_sum(q_f, q_f)
        inner = round_trip(r, rows, not last, fq_f)
        total = totals(r, rows)
        curvature = total[6:7, :]
        if step == 0:
            norm = total[7:8, :]
            cross = curvature
        else:
            cross = total[7:8, :]
        size = norm / curvature
        mult_ref[...] = mult_ref[...] + size * d_f[0 : 2 * lf, :]
        if last:
            for f in range(2):
                proj_ref[face(f), :] = p_f[face(f), :] + size * (q_f[face(f), :] - mode_image(f))
            break
        norm_next = norm + 2.0 * size * cross + size * size * (total[8:9, :] - inner)
        ratio = norm_next / norm
        for f in range(4):
            q = q_f[face(f), :]
            p = p_f[face(f), :] + size * (q - mode_image(f))
            p_f[face(f), :] = p
            fp = fp_f[face(f), :] + size * (fq_f[face(f), :] - dual_mode_image(f))
            fp_f[face(f), :] = fp
            d_f[face(f), :] = p + ratio * d_f[face(f), :]
            q_f[face(f), :] = fp + ratio * q
        norm = norm_next

    for copy in pending:
        copy.wait_send()
    for f in range(2):
        @pl.when(exists[f])
        def _():
            neighbour_copy(f, pack.at[f], nb_pack.at[f], pk_send.at[f], pk_recv.at[f]).wait_send()
            neighbour_copy(
                f, loads_hbm.at[face(f)], loads4.at[face(2 + f)], ld_send.at[f], ld_recv.at[f]
            ).wait_send()
    for f in range(4):
        @pl.when(exists[f])
        def _():
            for r in range(APPLIES):
                face_copy(r, f).wait_send()


def solution(mesh):
    nx, ny = mesh.shape["gx"], mesh.shape["gy"]

    def local(dual_ops, loads, coarse_rhs, coarse_modes, free_mask, face_match, coarse_rows):
        lm = dual_ops.shape[-1]
        lf, nc = loads.shape[-2:]
        wide = nx * ny * 8
        vmem = pl.BlockSpec(memory_space=pltpu.VMEM)
        hbm = pl.BlockSpec(memory_space=pl.ANY)
        dma = pltpu.SemaphoreType.DMA
        out = jax.ShapeDtypeStruct((2 * lf, nc), F32)
        field = pltpu.VMEM((lm, nc), F32)
        mult, proj = pl.pallas_call(
            functools.partial(kernel, nx, ny),
            out_shape=(out, out),
            in_specs=[hbm, hbm] + [vmem] * 5,
            out_specs=(vmem, vmem),
            scratch_shapes=[
                pltpu.VMEM((lm, lm), F32),
                pltpu.VMEM((lm, lm), BF16),
                pltpu.VMEM((lm, lm), BF16),
                field,
                pltpu.VMEM((2, 24, lf), F32),
                pltpu.VMEM((2, 24, lf), F32),
                pltpu.VMEM((nx, ny, 8, wide), F32),
                pltpu.VMEM((ROUNDS, nx, ny, 16, nc), F32),
                pltpu.VMEM((nx * ny, 8, nc), F32),
                pltpu.VMEM((5, nc, 2 * nc), F32),
                pltpu.VMEM((16, lm), F32),
                pltpu.VMEM((lm, nc), BF16),
                pltpu.VMEM((lm, nc), BF16),
                pltpu.VMEM((lm, 2 * nc), BF16),
                pltpu.VMEM((lm, 2 * nc), BF16),
                field,
                pltpu.VMEM((nc, lf), F32),
                pltpu.VMEM((2, lf, lf), BF16),
                pltpu.VMEM((2, lf, lf), BF16),
                pltpu.VMEM((lm, 2 * nc), BF16),
                pltpu.VMEM((lm, 2 * nc), BF16),
                pltpu.VMEM((APPLIES, 4, lf, nc), F32),
                pltpu.VMEM((APPLIES, 4, lf, nc), F32),
                field, field, field, field, field,
                dma((6,)),
                dma,
                dma((APPLIES, 4)),
                dma((APPLIES, 4)),
                dma((2,)), dma((2,)), dma((2,)), dma((2,)),
                dma((ROUNDS, ny)), dma((ROUNDS, ny)),
                dma((ROUNDS, nx)), dma((ROUNDS, nx)),
                dma((ny,)), dma((ny,)), dma((nx,)), dma((nx,)),
            ],
            compiler_params=pltpu.CompilerParams(
                collective_id=0, has_side_effects=True, vmem_limit_bytes=58 * 1024 * 1024
            ),
        )(
            dual_ops.reshape(lm, lm),
            loads.reshape(2 * lf, nc),
            coarse_rhs.reshape(coarse_rhs.shape[2:]),
            coarse_modes.reshape(coarse_modes.shape[2:]),
            free_mask.reshape(free_mask.shape[2:]),
            face_match.reshape(face_match.shape[2:]),
            coarse_rows.reshape(coarse_rows.shape[2:]),
        )
        return (mult.reshape(1, 1, 2, lf, nc), proj.reshape(1, 1, 2, lf, nc))

    in_specs = (
        P("gx", "gy", None, None),
        P("gx", "gy", None, None, None),
        P("gx", "gy", None, None),
        P("gx", "gy", None, None, None, None),
        P("gx", "gy", None, None),
        P("gx", "gy", None, None),
        P("gx", "gy", None, None, None),
    )
    out_specs = (P("gx", "gy", None, None, None), P("gx", "gy", None, None, None))
    return jax.shard_map(local, mesh=mesh, in_specs=in_specs, out_specs=out_specs, check_vma=False)
```

time: 711 us -> 76.8 us (0.11); the launches traced: 701 us -> 76.4 us
  blocking collectives: 470 us -> 0 us
  Pallas kernels: 0 us -> 68.2 us
  matrix products: 67.2 us -> 0 us
  local copies, waits for them, and re-layouts: 66.4 us -> 7.53 us
  waiting for transfers between devices: 34.1 us -> 0 us
  other arithmetic: 32.3 us -> 0 us
  starting transfers between devices: 29.1 us -> 0 us
    all_gather x5 -> x0, blocking collectives: 352 us -> none  [coarse_solve(): gathered = lax.all_gather(stacked, ('gx', 'gy'), axis=0, tiled=True)]
    psum x3 -> x0, blocking collectives: 118 us -> none  [local(): lax.psum((jnp.sum(direction * image, axis=(0, 1)), jnp.sum(projected * pr...]
    pallas_call x0 -> x1, Pallas kernels: none -> 68.2 us  [local(): pl.pallas_call(functools.partial(kernel, nx, ny), out_shape=(out, out), i...]
    dot_general x41 -> x0, matrix products: 67.2 us -> none  [the longest x4 48.9 us: apply_dual(): jnp.dot(operator, stacked, precision=HIGHEST, preferred_element_type=jnp....]
    ppermute x16 -> x0, waiting for transfers between devices: 34.1 us -> none  [shifted(): return lax.ppermute(shard, axis, pairs)]
    ppermute x16 -> x0, starting transfers between devices: 29.1 us -> none  [shifted(): return lax.ppermute(shard, axis, pairs)]
    gather x32 -> x0, local copies, waits for them, and re-layouts: 21.7 us -> none  [the longest x8 6.43 us: apply_dual(): back_west = shifted(jnp.take(product[2], inverse_west, axis=0), 'gy', -1)]
    another operation x15 -> x0, local copies, waits for them, and re-layouts: 12.5 us -> none  [the longest x6 8.7 us: mode_images(): return jnp.stack([east_face, south_face]) * free_slots]
  transfers between devices with their start and end apart: 16 -> 0, of which waited for: 9 -> 0; matrix products, arithmetic and copies ran while one was open for 3% -> 0% of each run, Pallas kernels for 0% -> 0%
where the time goes in v1:
time: 76.8 us; the launch traced here: 76.4 us
  Pallas kernels  68.2 us (89%)
  local copies, waits for them, and re-layouts  7.53 us (10%)
    pallas_call x1, Pallas kernels, local(): pl.pallas_call(functools.partial(kernel, nx, ny), out_shape=(out, out), i...  68.2 us
    unnamed x5, local copies, waits for them, and re-layouts  7.53 us

profile of v1, /device:TPU:0, one launch (start us, length us, event | category | flops | bytes accessed | tf_op | source)
XLA Modules:
  0.0 76.4 jit_solution(4307880075134642356)
XLA Ops:
  0.6 1.3 %copy.17 = f32[1,1,6,128]{3,2,1,0:T(8,128)} copy(f32[1,1,6,128]{3,1,2,0:T(1,128)} %param.9) | data formatting | bytes 6144
  1.9 1.3 %copy.16 = f32[1,1,3,6,192]{4,3,1,2,0:T(8,128)} copy(f32[1,1,3,6,192]{4,1,3,2,0:T(1,128)} %param.13) | data formatting | bytes 27648
  3.2 1.4 %copy.15 = f32[1,1,2,2,6,384]{5,4,3,2,1,0:T(8,128)} copy(f32[1,1,2,2,6,384]{5,3,4,2,1,0:T(2,128)} %param.10) | data formatting | bytes 73728 | tf_op args[3]
  4.6 68.2 %shard_map.86 = (f32[768,128]{1,0:T(8,128)}, f32[768,128]{1,0:T(8,128)}) custom-call(f32[1536,1536]{1,0:T(8,128)} %bitcast.15, f32[768,128]{1,0:T(8,128)} %bitcast.16, f32[6,128]{1,0:T(8,128)} %bitcast.21, f32[2,2,6,384]{3,2,1,0:T(8,128)} %bitcast.19, s32[2,384]{1,0:T(2,128)} %bitcast.22, s32[2,384]{1,0:T(2,128)} %bitcast.23, f32[3,6,192]{2,1,0:T(8,128)} %bitcast.20), custom_call_target="tpu_custom_call" | custom-call | tf_op jit(solution)/shard_map/pallas_call | solution.py:438
  72.9 1.8 %copy.20 = f32[1,1,2,384,128]{4,3,2,1,0:T(8,128)} copy(f32[1,1,2,384,128]{4,3,2,1,0:T(8,128)} %bitcast.18) | data formatting | bytes 786432
  74.6 1.8 %copy.21 = f32[1,1,2,384,128]{4,3,2,1,0:T(8,128)} copy(f32[1,1,2,384,128]{4,3,2,1,0:T(8,128)} %bitcast.17) | data formatting | bytes 786432

commit v2 on v1

--- a/solution.py
+++ b/solution.py
@@ -30,8 +30,8 @@
 def kernel(
     nx, ny, a_hbm, loads_hbm, rhs_ref, modes_ref, free_ref, match_ref, rows_ref,
     mult_ref, proj_ref,
-    a_stage, a_high, a_low, loads4, pack, nb_pack, inverse, terms, alphas, alpha_pair,
-    gt8, g_high, g_low, fg_high, fg_low, free4, put, perm, perm_back, vsplit, u_split,
+    a_stage, a_high, a_low, loads4, pack, nb_pack, own_rows, inverse, terms, alphas, alpha_pair,
+    gt8, g_pair, fg_pair, free4, put, perm, perm_back, vsplit, u_split,
     outbox, inbox, p_f, d_f, q_f, fp_f, fq_f,
     a_sem, l_sem, face_send, face_recv, pk_send, pk_recv, ld_send, ld_recv,
     gy_send, gy_recv, gx_send, gx_recv, cy_send, cy_recv, cx_send, cx_recv,
@@ -39,8 +39,9 @@
     lf = free_ref.shape[1]
     nc = mult_ref.shape[1]
     lm = a_high.shape[0]
-    ncoarse = rows_ref.shape[2]
+    ncoarse = rows_ref.shape[3]
     wide = inverse.shape[3]
+    half = g_pair.shape[1] // 2
     me_x = lax.axis_index("gx")
     me_y = lax.axis_index("gy")
     exists = (me_y < ny - 1, me_x < nx - 1, me_y > 0, me_x > 0)
@@ -73,21 +74,25 @@
 
     pack[...] = jnp.zeros_like(pack)
     for f in range(2):
-        pack[f, 0:6, :] = modes_ref[f, 0]
-        pack[f, 8:14, :] = modes_ref[f, 1]
+        for m in range(6):
+            pack[f, m : m + 1, :] = modes_ref[f, m, 0:1, :]
+            pack[f, 8 + m : 9 + m, :] = modes_ref[f, m, 1:2, :]
         pack[f, 16:17, :] = free_ref[f : f + 1, :].astype(F32)
 
     row = lax.broadcasted_iota(jnp.int32, (ncoarse, wide), 0)
     col = lax.broadcasted_iota(jnp.int32, (ncoarse, wide), 1)
     slot = jnp.bitwise_and(col, 7)
     spread = jnp.where((row == 6 * jnp.right_shift(col, 3) + slot) & (slot < 6), 1.0, 0.0)
-    inverse[me_x, me_y] = jnp.zeros((8, wide), F32)
-    inverse[me_x, me_y, 0:6, :] = jnp.dot(
-        rows_ref[0], spread.astype(F32), precision=lax.Precision.HIGHEST,
+    own_rows[...] = jnp.zeros_like(own_rows)
+    for m in range(6):
+        own_rows[m : m + 1, :] = rows_ref[0, m]
+    inverse[me_x, me_y] = jnp.dot(
+        own_rows[...], spread.astype(F32), precision=lax.Precision.HIGHEST,
         preferred_element_type=F32,
     )
     terms[0, me_x, me_y] = jnp.zeros((16, nc), F32)
-    terms[0, me_x, me_y, 0:6, :] = rhs_ref[...]
+    for m in range(6):
+        terms[0, me_x, me_y, m : m + 1, :] = rhs_ref[m]
 
     pl.semaphore_wait(barrier, nx + ny - 2)
 
@@ -212,8 +217,9 @@
         q_f[face(f), :] = jnp.transpose(put[...])
         free4[face(f), :] = jnp.transpose(jnp.broadcast_to(mask, (nc, lf)))
     high, low = split(q_f[...])
-    g_high[...] = high
-    g_low[...] = low
+    vsplit[:, 0:nc] = high
+    vsplit[:, nc : 2 * nc] = low
+    g_pair[...] = jnp.concatenate([high[:, 0:half], low[:, 0:half]], axis=1)
 
     def split_field(ref):
         high, low = split(ref[...])
@@ -244,7 +250,8 @@
             z = z + both[:, 0:nc] + both[:, nc : 2 * nc]
             if f >= 2:
                 high, low = split(z)
-                z = dot32(perm_back[f - 2], high) + dot32(perm_back[f - 2], low)
+                moved = dot32(perm_back[f - 2], jnp.concatenate([high, low], axis=1))
+                z = moved[:, 0:nc] + moved[:, nc : 2 * nc]
             outbox[r, f] = z
 
             @pl.when(exists[f])
@@ -288,19 +295,20 @@
             high, low = split(alphas[xx * ny + yy])
             alpha_pair[which, 8 * k : 8 * k + 8, 0:nc] = high.astype(F32)
             alpha_pair[which, 8 * k : 8 * k + 8, nc : 2 * nc] = low.astype(F32)
-
-    def product(left_high, left_low, right):
-        both = dot32(left_high, right)
-        return dot32(left_low, right[:, 0:nc]) + both[:, 0:nc] + both[:, nc : 2 * nc]
+            alpha_pair[which, half + 8 * k : half + 8 * k + 8, 0:nc] = high.astype(F32)
 
     def mode_image(f):
-        return product(
-            g_high[face(f), :], g_low[face(f), :], alpha_pair[0].astype(BF16)
-        )
+        right = alpha_pair[0].astype(BF16)
+        both = dot32(g_pair[face(f), :], right)
+        return both[:, 0:nc] + both[:, nc : 2 * nc]
 
     def dual_mode_image(f):
-        right = jnp.concatenate([alpha_pair[0], alpha_pair[f + 1]], axis=0).astype(BF16)
-        return product(fg_high[face(f), :], fg_low[face(f), :], right)
+        own, far = alpha_pair[0], alpha_pair[f + 1]
+        right = jnp.concatenate(
+            [own[0:half], far[0:half], own[half:], far[half:]], axis=0
+        ).astype(BF16)
+        both = dot32(fg_pair[face(f), :], right)
+        return both[:, 0:nc] + both[:, nc : 2 * nc]
 
     def own_sum(left, right):
         return jnp.sum(
@@ -312,8 +320,6 @@
 
     alpha_pair[...] = jnp.zeros_like(alpha_pair)
 
-    vsplit[:, 0:nc] = g_high[...]
-    vsplit[:, nc : 2 * nc] = g_low[...]
     apply_start(0, lambda: None)
     finish(rhs_row)
     finish(inv_row)
@@ -324,10 +330,11 @@
         face_arrived(0, f)
         sign = 1.0 if f < 2 else -1.0
         mask = free4[face(f), :] * sign
-        for half, values in enumerate((outbox[0, f] * mask, -inbox[0, f] * mask)):
-            high, low = split(values)
-            fg_high[face(f), half * nc : (half + 1) * nc] = high
-            fg_low[face(f), half * nc : (half + 1) * nc] = low
+        own_high, own_low = split(outbox[0, f] * mask)
+        far_high, far_low = split(-inbox[0, f] * mask)
+        fg_pair[face(f), :] = jnp.concatenate(
+            [part[:, 0:half] for part in (own_high, far_high, own_low, far_low)], axis=1
+        )
 
     l_copy.wait()
     for f in range(2):
@@ -423,6 +430,17 @@
                 face_copy(r, f).wait_send()
 
 
+def hand_over(mult_in, proj_in, mult_out, proj_out, sem):
+    copies = [
+        pltpu.make_async_copy(mult_in, mult_out, sem.at[0]),
+        pltpu.make_async_copy(proj_in, proj_out, sem.at[1]),
+    ]
+    for copy in copies:
+        copy.start()
+    for copy in copies:
+        copy.wait()
+
+
 def solution(mesh):
     nx, ny = mesh.shape["gx"], mesh.shape["gy"]
 
@@ -430,6 +448,7 @@
         lm = dual_ops.shape[-1]
         lf, nc = loads.shape[-2:]
         wide = nx * ny * 8
+        half = 64
         vmem = pl.BlockSpec(memory_space=pltpu.VMEM)
         hbm = pl.BlockSpec(memory_space=pl.ANY)
         dma = pltpu.SemaphoreType.DMA
@@ -447,15 +466,14 @@
                 field,
                 pltpu.VMEM((2, 24, lf), F32),
                 pltpu.VMEM((2, 24, lf), F32),
+                pltpu.VMEM((8, nx * ny * 6), F32),
                 pltpu.VMEM((nx, ny, 8, wide), F32),
                 pltpu.VMEM((ROUNDS, nx, ny, 16, nc), F32),
                 pltpu.VMEM((nx * ny, 8, nc), F32),
-                pltpu.VMEM((5, nc, 2 * nc), F32),
+                pltpu.VMEM((5, 2 * half, 2 * nc), F32),
                 pltpu.VMEM((16, lm), F32),
-                pltpu.VMEM((lm, nc), BF16),
-                pltpu.VMEM((lm, nc), BF16),
-                pltpu.VMEM((lm, 2 * nc), BF16),
-                pltpu.VMEM((lm, 2 * nc), BF16),
+                pltpu.VMEM((lm, 2 * half), BF16),
+                pltpu.VMEM((lm, 4 * half), BF16),
                 field,
                 pltpu.VMEM((nc, lf), F32),
                 pltpu.VMEM((2, lf, lf), BF16),
@@ -480,12 +498,19 @@
         )(
             dual_ops.reshape(lm, lm),
             loads.reshape(2 * lf, nc),
-            coarse_rhs.reshape(coarse_rhs.shape[2:]),
-            coarse_modes.reshape(coarse_modes.shape[2:]),
+            jnp.swapaxes(coarse_rhs[0], 0, 1),
+            jnp.swapaxes(coarse_modes[0, 0], 1, 2),
             free_mask.reshape(free_mask.shape[2:]),
             face_match.reshape(face_match.shape[2:]),
-            coarse_rows.reshape(coarse_rows.shape[2:]),
-        )
+            coarse_rows[0, 0][:, :, None, :],
+        )
+        mult, proj = pl.pallas_call(
+            hand_over,
+            out_shape=(out, out),
+            in_specs=[hbm, hbm],
+            out_specs=(hbm, hbm),
+            scratch_shapes=[dma((2,))],
+        )(mult, proj)
         return (mult.reshape(1, 1, 2, lf, nc), proj.reshape(1, 1, 2, lf, nc))
 
     in_specs = (

time: 76.8 us -> 93.4 us (1.22)
  Pallas kernels: 68.2 us -> 92.4 us
  local copies, waits for them, and re-layouts: 7.53 us -> 0 us
    pallas_call x0 -> x1, Pallas kernels: none -> 24.9 us  [local(): pl.pallas_call(hand_over, out_shape=(out, out), in_specs=[hbm, hbm], out_...]
    unnamed x5 -> x0, local copies, waits for them, and re-layouts: 7.53 us -> none
where the time goes in v2:
time: 93.4 us; the launch traced here: 93.2 us
  Pallas kernels  92.4 us (99%)
    pallas_call x1, Pallas kernels, local(): pl.pallas_call(functools.partial(kernel, nx, ny), out_shape=(out, out), i...  67.5 us
    pallas_call x1, Pallas kernels, local(): pl.pallas_call(hand_over, out_shape=(out, out), in_specs=[hbm, hbm], out_...  24.9 us

profile of v2, /device:TPU:0, one launch (start us, length us, event | category | flops | bytes accessed | tf_op | source)
XLA Modules:
  0.0 93.2 jit_solution(5538394233169225372)
XLA Ops:
  0.6 67.5 %shard_map.86 = (f32[768,128]{1,0:T(8,128)}, f32[768,128]{1,0:T(8,128)}) custom-call(f32[1536,1536]{1,0:T(8,128)} %bitcast.11, f32[768,128]{1,0:T(8,128)} %bitcast.12, f32[6,1,128]{2,1,0:T(1,128)} %bitcast.15, f32[2,6,2,384]{3,2,1,0:T(2,128)} %bitcast.13, s32[2,384]{1,0:T(2,128)} %bitcast.16, s32[2,384]{1,0:T(2,128)} %bitcast.17, f32[3,6,1,192]{3,2,1,0:T(1,128)} %bitcast.14), custom_call_target="tpu_custom_call" | custom-call | tf_op jit(solution)/shard_map/pallas_call | solution.py:457
  68.1 24.9 %shard_map.87 = (f32[768,128]{1,0:T(8,128)}, f32[768,128]{1,0:T(8,128)}) custom-call(f32[768,128]{1,0:T(8,128)} %get-tuple-element.6.mult_in, f32[768,128]{1,0:T(8,128)} %get-tuple-element.7.proj_in), custom_call_target="tpu_custom_call" | custom-call | tf_op jit(solution)/shard_map/pallas_call | solution.py:507
